TPU v7x, 256 devices: a whole 4x4x8 slice. The times are simulated.
256 devices in a mesh: section: 4 (over z_hi), seq: 64 (over x, y, z_lo, core).
Axes of the slice: x: 4, y: 4, z: 8 (z_hi: 4, z_lo: 2; z = z_hi * 2 + z_lo), core: 2. Of those that a mesh axis runs over, the one named last changes fastest.
Arguments:
- memory: bfloat16 [8, 4096, 4096], P(None, 'seq', 'section'), may hold values from -6 to 6
- kv_weight: bfloat16 [4096, 4096], P('seq', 'section'), may hold values from -0.09375 to 0.09375
- mem_lengths: int32 [8], replicated, may hold values from 1024 to 4096, as said below
- queries: bfloat16 [16384, 2048], P('seq', 'section'), may hold values from -128 to 128
- out_weight: bfloat16 [2048, 4096], P('section'), may hold values from -0.125 to 0.125
- residual: bfloat16 [16384, 4096], P(('seq', 'section')), may hold values from -1.5 to 1.5
- norm_gain: float32 [4096], replicated, may hold values from 0.5 to 1.5
Outputs:
- hidden_out: bfloat16 [16384, 4096], P(('seq', 'section'))
- normed_out: bfloat16 [16384, 4096], P(('seq', 'section'))
Inputs may be any that keep to these rules, and one draw needn't show every extreme that they name: `mem_lengths`: valid memory positions of each proof state; positions at or beyond it are padding; at least one proof state has none.
All inputs are finite; a program needn't handle non-finite values.
Results may differ from a plain program's by a relative error of at most 0.012.
Values may be sent and summed in bfloat16 or wider, within the bound.
No kernel may reach another device: no remote copies, remote signals or barrier semaphores. Data moves between devices by JAX's collectives and lax.ppermute only.
A program may use at most 128 MiB of HBM per device.

v0:
```python
import math
import jax
import jax.numpy as jnp
from jax import lax
from jax.sharding import PartitionSpec as P

DH = 256


def project_rows(mem_rows, kv_weight):
    summed = jnp.dot(
        mem_rows,
        lax.all_gather(kv_weight, "seq", axis=0, tiled=True),
        preferred_element_type=jnp.float32,
    )
    return summed.astype(jnp.bfloat16)


def shards(memory, kv_weight, mem_lengths, queries, out_weight, residual, norm_gain):
    seq_count = lax.axis_size("seq")
    states = memory.shape[0]
    group = seq_count // states
    local_heads = queries.shape[1] // DH
    widened = lax.all_gather(memory, "section", axis=2, tiled=True)
    block_len = widened.shape[1]
    feature_count = widened.shape[2]
    projected = project_rows(widened.reshape(states * block_len, feature_count), kv_weight)
    projected = projected.reshape(states, block_len, projected.shape[1])
    spread = jnp.repeat(projected, group, axis=0)
    key_value = lax.all_to_all(spread, "seq", split_axis=0, concat_axis=1, tiled=True)[0]
    state_index = lax.axis_index("seq") // group
    length = lax.dynamic_index_in_dim(mem_lengths, state_index, 0, keepdims=False)
    memory_len = key_value.shape[0]
    split_heads = key_value.reshape(memory_len, local_heads, 2, DH)
    shard_key_rows = split_heads[:, :, 0, :]
    shard_value_rows = split_heads[:, :, 1, :]
    query_per_head = queries.reshape(queries.shape[0], local_heads, DH)
    logit_scores = jnp.einsum(
        "wac,oac->awo", query_per_head, shard_key_rows, preferred_element_type=jnp.float32
    )
    logit_scores = logit_scores * (1.0 / math.sqrt(DH))
    visible = jnp.arange(memory_len, dtype=jnp.int32) < length
    logit_scores = jnp.where(visible[None, None, :], logit_scores, -1e30)
    highest = jnp.max(logit_scores, axis=-1, keepdims=True)
    expo = jnp.exp(logit_scores - highest)
    softmax_weight = (expo / jnp.sum(expo, axis=-1, keepdims=True)).astype(jnp.bfloat16)
    attended_context = jnp.einsum(
        "fsw,wfy->sfy", softmax_weight, shard_value_rows, preferred_element_type=jnp.float32
    )
    attended_context = attended_context.astype(jnp.bfloat16).reshape(
        query_per_head.shape[0], local_heads * DH
    )
    attended = lax.psum_scatter(
        jnp.dot(attended_context, out_weight, preferred_element_type=jnp.float32),
        "section",
        scatter_dimension=0,
        tiled=True,
    )
    combined = residual.astype(jnp.float32) + attended
    mean_square = jnp.mean(combined * combined, axis=-1, keepdims=True)
    normed = combined * lax.rsqrt(mean_square + 1e-06) * norm_gain
    return (combined.astype(jnp.bfloat16), normed.astype(jnp.bfloat16))


def solution(mesh):
    in_specs = (
        P(None, "seq", "section"),
        P("seq", "section"),
        P(),
        P("seq", "section"),
        P("section", None),
        P(("seq", "section"), None),
        P(),
    )
    out_specs = (P(("seq", "section"), None), P(("seq", "section"), None))
    return jax.shard_map(shards, mesh=mesh, in_specs=in_specs, out_specs=out_specs, check_vma=False)
```

profile of v0, /device:TPU:1, one launch (start us, length us, event | category | flops | bytes accessed | tf_op | source)
XLA Modules:
  0.0 516.3 jit_solution(13996166611527082985)
XLA Ops:
  7.2 0.0 all-gather.3.cloned.1.call-start
  7.2 0.7 all-gather.3.cloned.1.call-update
  7.9 0.0 all-gather.5.cloned.1.call-start
  7.9 0.7 all-gather.5.cloned.1.call-update
  8.6 80.3 %all-gather.3.cloned.1.call-done = bf16[8,64,4096]{2,1,0:T(8,128)(2,1)} async-done(((bf16[8,64,1024]{2,1,0:T(8,128)(2,1)}), bf16[8,64,4096]{2,1,0:T(8,128)(2,1)}) %all-gather.3.cloned.1.call-update) | async-done | bytes 4194320 | tf_op jit(solution)/shard_map/all_gather | solution.py:24
  89.0 124.5 %all-gather.5.cloned.1.call-done = bf16[4096,1024]{1,0:T(8,128)(2,1)} async-done(((bf16[64,1024]{1,0:T(8,128)(2,1)}), bf16[4096,1024]{1,0:T(8,128)(2,1)}) %all-gather.5.cloned.1.call-update) | async-done | bytes 8388624 | tf_op jit(solution)/shard_map/all_gather | solution.py:13
  213.5 9.1 %convolution_convert_fusion = bf16[512,1024]{1,0:T(8,128)(2,1)S(1)} fusion(bf16[512,4096]{1,0:T(8,128)(2,1)} %bitcast.38, bf16[4096,1024]{1,0:T(8,128)(2,1)} %all-gather.5.cloned.1.call-done), kind=kOutput, calls=%fused_computation.14 | convolution fusion | flops 4295491584 | bytes 13631488 | tf_op jit(solution)/shard_map/dot_general | solution.py:11
  222.6 4.3 broadcast_in_dim.20
  226.9 0.0 copy-start.5
  226.9 6.5 %all-to-all-start = ((bf16[64,64,1024]{2,1,0:T(8,128)(2,1)}), bf16[64,64,1024]{2,1,0:T(8,128)(2,1)}, u32[]{:S(2)}, u32[]{:S(2)}) async-start(bf16[64,64,1024]{2,1,0:T(8,128)(2,1)} %bitcast.34), calls=%async_computation | async-start | bytes 16777216 | tf_op jit(solution)/shard_map/all_to_all | solution.py:30
  233.5 0.2 reduce-scatter.2.cloned.1.call-start
  233.7 0.0 copy-done.5
  233.7 0.6 dynamic_slice.4
  234.3 0.7 iota_compare_fusion
  235.0 102.5 %all-to-all-done = bf16[64,64,1024]{2,1,0:T(8,128)(2,1)} async-done(((bf16[64,64,1024]{2,1,0:T(8,128)(2,1)}), bf16[64,64,1024]{2,1,0:T(8,128)(2,1)}, u32[]{:S(2)}, u32[]{:S(2)}) %all-to-all-start) | async-done | bytes 8388640 | tf_op jit(solution)/shard_map/all_to_all | solution.py:30
  337.5 14.5 %reshape_squeeze.3 = bf16[4096,2,2,256]{3,2,1,0:T(2,128)(2,1)} reshape(bf16[64,64,1024]{2,1,0:T(8,128)(2,1)} %all-to-all-done) | data formatting | bytes 16777216 | tf_op jit(solution)/shard_map/reshape;squeeze | solution.py:34
  351.9 17.3 %fusion.19 = (bf16[4096,2,1,256]{3,2,1,0:T(2,128)(2,1)}, bf16[4096,2,1,256]{3,2,1,0:T(2,128)(2,1)}) fusion(bf16[4096,2,2,256]{3,2,1,0:T(2,128)(2,1)} %reshape_squeeze.3), kind=kLoop, calls=%fused_computation.26 | loop fusion | bytes 16777216 | tf_op jit(solution)/shard_map/slice | solution.py:36
  369.3 0.0 copy-start.3
  369.3 18.5 %copy.17 = bf16[4096,2,1,256]{0,3,1,2:T(8,128)(2,1)} copy(bf16[4096,2,1,256]{3,2,1,0:T(2,128)(2,1)} %get-tuple-element.2) | data formatting | bytes 8388608
  387.8 0.0 copy-done.3
  387.8 4.7 fusion.5
  392.4 0.0 copy-start.1
  392.5 6.0 %fusion.20 = (f32[2,256]{1,0:T(2,128)S(1)}, f32[2,256,4096]{1,2,0:T(8,128)}) fusion(f32[2,4096,256]{2,1,0:T(8,128)S(1)} %fusion.5, pred[4096]{0:T(1024)(128)(4,1)S(1)} %iota_compare_fusion), kind=kOutput, calls=%fused_computation.27 | output fusion | flops 12587007 | bytes 16783360 | tf_op jit(solution)/shard_map/sub | solution.py:45
  398.5 0.0 copy-done.1
  398.5 0.0 copy-start
  398.5 4.9 fusion.11
  403.4 0.0 copy-start.2
  403.4 0.0 copy-start.4
  403.4 0.0 copy-done
  403.4 3.2 fusion.21
  406.6 0.0 reduce-scatter.2.cloned.1.call-update
  406.7 99.2 %reduce-scatter.2.cloned.1.call-done = f32[64,4096]{1,0:T(8,128)} async-done(((f32[256,4096]{1,0:T(8,128)}), f32[64,4096]{1,0:T(8,128)}) %reduce-scatter.2.cloned.1.call-update) | async-done | bytes 1048592 | tf_op jit(solution)/shard_map/reduce_scatter | solution.py:53
  505.8 0.0 copy-done.2
  505.8 1.5 multiply_reduce_fusion
  507.3 0.0 copy-done.4
  507.3 2.4 multiply_convert_fusion
  (1 shorter events, 0.0 us)
Async XLA Ops:
  7.2 81.8 %all-gather.3.cloned.1.call-start = ((), (), s32[]{:S(2)}) async-start(), calls=%async_computation.2 | async-start | bytes 5242880 | tf_op jit(solution)/shard_map/all_gather | solution.py:24
  7.9 205.6 %all-gather.5.cloned.1.call-start = ((), (), s32[]{:S(2)}) async-start(), calls=%async_computation.3 | async-start | bytes 8519680 | tf_op jit(solution)/shard_map/all_gather | solution.py:13
  226.9 6.8 %copy-start.5 = (s32[8]{0:T(128)S(1)}, s32[8]{0:T(128)}, u32[]{:S(2)}) copy-start(s32[8]{0:T(128)} %param.9) | copy-start | bytes 100
  226.9 110.5 %all-to-all-start = ((bf16[64,64,1024]{2,1,0:T(8,128)(2,1)}), bf16[64,64,1024]{2,1,0:T(8,128)(2,1)}, u32[]{:S(2)}, u32[]{:S(2)}) async-start(bf16[64,64,1024]{2,1,0:T(8,128)(2,1)} %bitcast.34), calls=%async_computation | async-start | bytes 16777216 | tf_op jit(solution)/shard_map/all_to_all | solution.py:30
  233.5 272.4 %reduce-scatter.2.cloned.1.call-start = ((), (), s32[]{:S(2)}) async-start(), calls=%async_computation.4 | async-start | bytes 5242880 | tf_op jit(solution)/shard_map/reduce_scatter | solution.py:53
  369.3 18.5 %copy-start.3 = (bf16[256,512]{1,0:T(8,128)(2,1)S(1)}, bf16[256,512]{1,0:T(8,128)(2,1)}, u32[]{:S(2)}) copy-start(bf16[256,512]{1,0:T(8,128)(2,1)} %param.10) | copy-start | bytes 786436
  392.4 6.0 %copy-start.1 = (bf16[4096,2,1,256]{0,3,1,2:T(8,128)(2,1)S(1)}, bf16[4096,2,1,256]{0,3,1,2:T(8,128)(2,1)}, u32[]{:S(2)}) copy-start(bf16[4096,2,1,256]{0,3,1,2:T(8,128)(2,1)} %copy.17) | copy-start | bytes 12582916
  398.5 4.9 copy-start
  403.4 102.5 %copy-start.2 = (bf16[64,4096]{1,0:T(8,128)(2,1)S(1)}, bf16[64,4096]{1,0:T(8,128)(2,1)}, u32[]{:S(2)}) copy-start(bf16[64,4096]{1,0:T(8,128)(2,1)} %param.12) | copy-start | bytes 1572868
  403.4 104.0 %copy-start.4 = (f32[4096]{0:T(1024)S(1)}, f32[4096]{0:T(1024)}, u32[]{:S(2)}) copy-start(f32[4096]{0:T(1024)} %param.13) | copy-start | bytes 49156
Sparse Core Ops, SparseCore 0:
  9.8 79.1 all-gather.2
  90.8 122.6 all-gather.4
  406.8 99.0 reduce-scatter.1
where the time goes:
time: 517 us; the launch traced here: 516 us
  waiting for transfers between devices  408 us (79%)
  local copies, waits for them, and re-layouts  55.2 us (11%)
  matrix products  21.9 us (4%)
  between operations  13.9 us (3%)
  other arithmetic  10.5 us (2%)
  starting transfers between devices  6.81 us (1%)
    all_gather x1, waiting for transfers between devices, project_rows(): lax.all_gather(kv_weight, 'seq', axis=0, tiled=True)  125 us
    all_to_all x1, waiting for transfers between devices, shards(): lax.all_to_all(spread, 'seq', split_axis=0, concat_axis=1, tiled=True)[0]  102 us
    reduce_scatter x1, waiting for transfers between devices, shards(): lax.psum_scatter(jnp.dot(attended_context, out_weight, preferred_element_...  99.2 us
    all_gather x1, waiting for transfers between devices, shards(): widened = lax.all_gather(memory, 'section', axis=2, tiled=True)  80.3 us
    unnamed x13, local copies, waits for them, and re-layouts  18.5 us
    slice x1, local copies, waits for them, and re-layouts, shards(): shard_value_rows = split_heads[:, :, 1, :]  17.3 us
    another operation x1, local copies, waits for them, and re-layouts, shards(): split_heads = key_value.reshape(memory_len, local_heads, 2, DH)  14.5 us
  transfers between devices with their start and end apart: 4, of which 4 were waited for; matrix products, arithmetic and copies ran while one was open for 0% of the time, Pallas kernels for 0%

commit v1 on v0

--- a/solution.py
+++ b/solution.py
@@ -21,7 +21,9 @@
     states = memory.shape[0]
     group = seq_count // states
     local_heads = queries.shape[1] // DH
-    widened = lax.all_gather(memory, "section", axis=2, tiled=True)
+    widened = jnp.concatenate(
+        lax.all_to_all(jnp.stack([memory] * lax.axis_size("section")), "section", 0, 0), axis=2
+    )
     block_len = widened.shape[1]
     feature_count = widened.shape[2]
     projected = project_rows(widened.reshape(states * block_len, feature_count), kv_weight)

time: 517 us -> 462 us (0.89)
  waiting for transfers between devices: 408 us -> 198 us
  blocking collectives: 0 us -> 144 us
  local copies, waits for them, and re-layouts: 55.2 us -> 64.3 us
    all_to_all x0 -> x1, blocking collectives: none -> 144 us  [shards(): lax.all_to_all(jnp.stack([memory] * lax.axis_size('section')), 'section',...]
    all_gather x1, waiting for transfers between devices: 125 us -> 0.01 us  [project_rows(): lax.all_gather(kv_weight, 'seq', axis=0, tiled=True)]
    all_gather x1 -> x0, waiting for transfers between devices: 80.3 us -> none  [shards(): widened = lax.all_gather(memory, 'section', axis=2, tiled=True)]
    reduce_scatter x1, waiting for transfers between devices: 99.2 us -> 94 us  [shards(): lax.psum_scatter(jnp.dot(attended_context, out_weight, preferred_element_...]
    unnamed x13 -> x14, local copies, waits for them, and re-layouts: 18.5 us -> 22.8 us
  transfers between devices with their start and end apart: 4 -> 3, of which waited for: 4 -> 2; matrix products, arithmetic and copies ran while one was open for 0% -> 2% of each run, Pallas kernels for 0% -> 0%
where the time goes in v1:
time: 462 us; the launch traced here: 461 us
  waiting for transfers between devices  198 us (43%)
  blocking collectives  144 us (31%)
  local copies, waits for them, and re-layouts  64.3 us (14%)
  matrix products  21.9 us (5%)
  between operations  14.2 us (3%)
  other arithmetic  10.5 us (2%)
  starting transfers between devices  8.85 us (2%)
    all_to_all x1, blocking collectives, shards(): lax.all_to_all(jnp.stack([memory] * lax.axis_size('section')), 'section',...  144 us
    all_to_all x1, waiting for transfers between devices, shards(): lax.all_to_all(spread, 'seq', split_axis=0, concat_axis=1, tiled=True)[0]  103 us
    reduce_scatter x1, waiting for transfers between devices, shards(): lax.psum_scatter(jnp.dot(attended_context, out_weight, preferred_element_...  94 us
    unnamed x14, local copies, waits for them, and re-layouts  22.8 us
    slice x1, local copies, waits for them, and re-layouts, shards(): shard_value_rows = split_heads[:, :, 1, :]  17.2 us
    another operation x1, local copies, waits for them, and re-layouts, shards(): split_heads = key_value.reshape(memory_len, local_heads, 2, DH)  14.4 us
  transfers between devices with their start and end apart: 3, of which 2 were waited for; matrix products, arithmetic and copies ran while one was open for 2% of the time, Pallas kernels for 0%

profile of v1, /device:TPU:1, one launch (start us, length us, event | category | flops | bytes accessed | tf_op | source)
XLA Modules:
  0.0 461.2 jit_solution(2233285493416272345)
XLA Ops:
  7.2 0.0 all-gather.2.cloned.1.call-start
  7.2 0.7 all-gather.2.cloned.1.call-update
  7.9 1.7 stack.2
  9.6 143.8 %all_to_all.14 = bf16[4,8,64,1024]{3,2,1,0:T(8,128)(2,1)S(1)} all-to-all(bf16[4,8,64,1024]{3,2,1,0:T(8,128)(2,1)S(1)} %stack.2), channel_id=1, replica_groups=mesh['section'=4,'seq'=64] {'section'}, dimensions={0} | all-to-all | bytes 8388608 | tf_op jit(solution)/shard_map/all_to_all | solution.py:25
  153.5 3.3 copy.16
  156.7 4.3 copy.25
  161.0 0.0 all-gather.2.cloned.1.call-done
  161.0 9.1 %convolution_convert_fusion = bf16[512,1024]{1,0:T(8,128)(2,1)S(1)} fusion(bf16[512,4096]{1,0:T(8,128)(2,1)} %bitcast.40, bf16[4096,1024]{1,0:T(8,128)(2,1)} %all-gather.2.cloned.1.call-done), kind=kOutput, calls=%fused_computation.14 | convolution fusion | flops 4295491584 | bytes 13631488 | tf_op jit(solution)/shard_map/dot_general | solution.py:11
  170.2 4.3 broadcast_in_dim.20
  174.5 0.0 copy-start.5
  174.5 8.6 %all-to-all-start.1 = ((bf16[64,64,1024]{2,1,0:T(8,128)(2,1)}), bf16[64,64,1024]{2,1,0:T(8,128)(2,1)}, u32[]{:S(2)}, u32[]{:S(2)}) async-start(bf16[64,64,1024]{2,1,0:T(8,128)(2,1)} %bitcast.37), calls=%async_computation.1 | async-start | bytes 16777216 | tf_op jit(solution)/shard_map/all_to_all | solution.py:32
  183.1 0.2 reduce-scatter.2.cloned.1.call-start
  183.3 0.0 copy-done.5
  183.3 0.6 dynamic_slice.4
  183.9 0.7 iota_compare_fusion
  184.6 102.9 %all-to-all-done.1 = bf16[64,64,1024]{2,1,0:T(8,128)(2,1)} async-done(((bf16[64,64,1024]{2,1,0:T(8,128)(2,1)}), bf16[64,64,1024]{2,1,0:T(8,128)(2,1)}, u32[]{:S(2)}, u32[]{:S(2)}) %all-to-all-start.1) | async-done | bytes 8388640 | tf_op jit(solution)/shard_map/all_to_all | solution.py:32
  287.5 14.4 %reshape_squeeze.3 = bf16[4096,2,2,256]{3,2,1,0:T(2,128)(2,1)} reshape(bf16[64,64,1024]{2,1,0:T(8,128)(2,1)} %all-to-all-done.1) | data formatting | bytes 16777216 | tf_op jit(solution)/shard_map/reshape;squeeze | solution.py:36
  301.9 17.2 %fusion.19 = (bf16[4096,2,1,256]{3,2,1,0:T(2,128)(2,1)}, bf16[4096,2,1,256]{3,2,1,0:T(2,128)(2,1)}) fusion(bf16[4096,2,2,256]{3,2,1,0:T(2,128)(2,1)} %reshape_squeeze.3), kind=kLoop, calls=%fused_computation.26 | loop fusion | bytes 16777216 | tf_op jit(solution)/shard_map/slice | solution.py:38
  319.1 0.0 copy-start.3
  319.1 18.4 %copy.22 = bf16[4096,2,1,256]{0,3,1,2:T(8,128)(2,1)} copy(bf16[4096,2,1,256]{3,2,1,0:T(2,128)(2,1)} %get-tuple-element.2) | data formatting | bytes 8388608
  337.6 0.0 copy-done.3
  337.6 4.7 %fusion.5 = f32[2,4096,256]{2,1,0:T(8,128)S(1)} fusion(bf16[4096,2,1,256]{3,2,1,0:T(2,128)(2,1)} %get-tuple-element.3, bf16[32,2,8,256]{3,2,1,0:T(8,128)(2,1)S(1)} %bitcast.43), kind=kOutput, calls=%fused_computation.8 | convolution fusion | flops 1073741824 | bytes 12845056 | tf_op jit(solution)/shard_map/wac,oac->awo/dot_general | solution.py:40
  342.3 0.0 copy-start.1
  342.3 6.0 %fusion.20 = (f32[2,256]{1,0:T(2,128)S(1)}, f32[2,256,4096]{1,2,0:T(8,128)}) fusion(f32[2,4096,256]{2,1,0:T(8,128)S(1)} %fusion.5, pred[4096]{0:T(1024)(128)(4,1)S(1)} %iota_compare_fusion), kind=kOutput, calls=%fused_computation.27 | output fusion | flops 12587007 | bytes 16783360 | tf_op jit(solution)/shard_map/sub | solution.py:47
  348.3 0.0 copy-done.1
  348.3 0.0 copy-start
  348.3 4.9 %fusion.11 = bf16[2,256,256]{2,1,0:T(8,128)(2,1)S(1)} fusion(f32[2,256,4096]{1,2,0:T(8,128)} %get-tuple-element.7, f32[2,256]{1,0:T(2,128)S(1)} %get-tuple-element.6, bf16[4096,2,1,256]{0,3,1,2:T(8,128)(2,1)S(1)} %copy-done.1), kind=kOutput, calls=%fused_computation.15 | convolution fusion | flops 1078067200 | bytes 12847104 | tf_op jit(solution)/shard_map/fsw,wfy->sfy/dot_general | solution.py:49
  353.2 0.0 copy-start.2
  353.2 0.0 copy-start.4
  353.2 0.0 copy-done
  353.2 3.2 fusion.21
  356.5 0.0 reduce-scatter.2.cloned.1.call-update
  356.5 94.0 %reduce-scatter.2.cloned.1.call-done = f32[64,4096]{1,0:T(8,128)} async-done(((f32[256,4096]{1,0:T(8,128)}), f32[64,4096]{1,0:T(8,128)}) %reduce-scatter.2.cloned.1.call-update) | async-done | bytes 1048592 | tf_op jit(solution)/shard_map/reduce_scatter | solution.py:55
  450.5 0.0 copy-done.2
  450.5 1.5 multiply_reduce_fusion
  452.0 0.0 copy-done.4
  452.0 2.4 multiply_convert_fusion
  (1 shorter events, 0.0 us)
Async XLA Ops:
  7.2 153.9 %all-gather.2.cloned.1.call-start = ((), (), s32[]{:S(2)}) async-start(), calls=%async_computation.3 | async-start | bytes 8519680 | tf_op jit(solution)/shard_map/all_gather | solution.py:13
  174.5 8.8 %copy-start.5 = (s32[8]{0:T(128)S(1)}, s32[8]{0:T(128)}, u32[]{:S(2)}) copy-start(s32[8]{0:T(128)} %param.9) | copy-start | bytes 100
  174.5 113.0 %all-to-all-start.1 = ((bf16[64,64,1024]{2,1,0:T(8,128)(2,1)}), bf16[64,64,1024]{2,1,0:T(8,128)(2,1)}, u32[]{:S(2)}, u32[]{:S(2)}) async-start(bf16[64,64,1024]{2,1,0:T(8,128)(2,1)} %bitcast.37), calls=%async_computation.1 | async-start | bytes 16777216 | tf_op jit(solution)/shard_map/all_to_all | solution.py:32
  183.1 267.4 %reduce-scatter.2.cloned.1.call-start = ((), (), s32[]{:S(2)}) async-start(), calls=%async_computation.4 | async-start | bytes 5242880 | tf_op jit(solution)/shard_map/reduce_scatter | solution.py:55
  319.1 18.5 %copy-start.3 = (bf16[256,512]{1,0:T(8,128)(2,1)S(1)}, bf16[256,512]{1,0:T(8,128)(2,1)}, u32[]{:S(2)}) copy-start(bf16[256,512]{1,0:T(8,128)(2,1)} %param.10) | copy-start | bytes 786436
  342.3 6.0 %copy-start.1 = (bf16[4096,2,1,256]{0,3,1,2:T(8,128)(2,1)S(1)}, bf16[4096,2,1,256]{0,3,1,2:T(8,128)(2,1)}, u32[]{:S(2)}) copy-start(bf16[4096,2,1,256]{0,3,1,2:T(8,128)(2,1)} %copy.22) | copy-start | bytes 12582916
  348.3 4.9 %copy-start = (bf16[512,4096]{1,0:T(8,128)(2,1)S(1)}, bf16[512,4096]{1,0:T(8,128)(2,1)}, u32[]{:S(2)}) copy-start(bf16[512,4096]{1,0:T(8,128)(2,1)} %param.11) | copy-start | bytes 12582916
  353.2 97.3 %copy-start.2 = (bf16[64,4096]{1,0:T(8,128)(2,1)S(1)}, bf16[64,4096]{1,0:T(8,128)(2,1)}, u32[]{:S(2)}) copy-start(bf16[64,4096]{1,0:T(8,128)(2,1)} %param.12) | copy-start | bytes 1572868
  353.2 98.8 %copy-start.4 = (f32[4096]{0:T(1024)S(1)}, f32[4096]{0:T(1024)}, u32[]{:S(2)}) copy-start(f32[4096]{0:T(1024)} %param.13) | copy-start | bytes 49156
Sparse Core Ops, SparseCore 0:
  9.8 148.9 all-gather.1
  356.6 93.8 reduce-scatter.1
